TPU v7x, 256 devices: a whole 4x4x8 slice. The times are simulated.
256 devices in a mesh: prefix: 8 (over z), feat: 32 (over y, x, core).
Axes of the slice: x: 4, y: 4, z: 8, core: 2. Of those that a mesh axis runs over, the one named last changes fastest.
Arguments:
- activations: float32 [1024, 1152], P('feat'), may hold values from -6 to 6
- enc_weight: float32 [16, 9216, 1152], P('prefix', 'feat'), may hold values from -0.1875 to 0.1875
- dec_weight: float32 [16, 9216, 1152], P('prefix', 'feat'), may hold values from -0.0625 to 0.0625
Outputs:
- enc_grad: float32 [16, 9216, 1152], P('prefix', 'feat')
- dec_grad: float32 [16, 9216, 1152], P('prefix', 'feat')
All inputs are finite; a program needn't handle non-finite values.
Results may differ from a plain program's by a relative error of at most 0.000094.
Values sent between devices are 32-bit elements; how exact they have to be, the bound alone decides.
No kernel may reach another device: no remote copies, remote signals or barrier semaphores. Data moves between devices by JAX's collectives and lax.ppermute only.
A program may use at most 128 MiB of HBM per device.

v0:
```python
import jax
import jax.numpy as jnp
from jax import lax
from jax.sharding import PartitionSpec as P

HIGHEST = lax.Precision.HIGHEST


def entering(shard, axis, combine, identity, reverse):
    count, here = (lax.axis_size(axis), lax.axis_index(axis))
    everything = lax.all_gather(shard, axis)
    start = jnp.broadcast_to(jnp.asarray(identity, shard.dtype), shard.shape)

    def step(k, before):
        at = count - 1 - k if reverse else k
        reached = at > here if reverse else at < here
        new = combine(before, everything[at])
        return jnp.where(reached, new, before)

    return lax.fori_loop(0, count, step, start)


def add_terms(earlier, later):
    return earlier + later


def chain_scan(decoded, act_rows):
    group_total = jnp.sum(decoded, axis=1)
    nothing = jnp.zeros_like(group_total)
    before = entering(group_total, "prefix", add_terms, nothing, False)
    rebuilt = before[:, None, :] + jnp.cumsum(decoded, axis=1)
    errors = rebuilt - act_rows[:, None, :]
    error_total = jnp.sum(errors, axis=1)
    beyond = entering(error_total, "prefix", add_terms, nothing, True)
    return beyond[:, None, :] + jnp.flip(jnp.cumsum(jnp.flip(errors, 1), axis=1), 1)


def per_device(activations, enc_weight, dec_weight):
    local_groups, local_feats, model_width = enc_weight.shape
    gathered = lax.all_gather(activations, "feat", axis=0, tiled=True)
    tokens = gathered.shape[0]
    pre_act = jnp.einsum("nd,gkd->gnk", gathered, enc_weight, precision=HIGHEST)
    features = jax.nn.softplus(4.0 * pre_act) / 4.0
    slopes = jax.nn.sigmoid(4.0 * pre_act)
    factor = 2.0 / tokens
    empty = jnp.zeros(enc_weight.shape, jnp.float32)
    own_rows = tokens // lax.axis_size("feat")
    feat_rows = features
    product = jnp.einsum("gnk,gkd->ngd", feat_rows, dec_weight, precision=HIGHEST)
    summed = lax.psum_scatter(
        product.reshape(lax.axis_size("feat") * own_rows, local_groups * model_width),
        "feat",
        scatter_dimension=0,
        tiled=True,
    )
    decoded = summed.reshape(summed.shape[0], local_groups, model_width)
    suffix = factor * chain_scan(decoded, activations)
    suffix_piece = lax.all_gather(suffix, "feat", axis=0, tiled=True)
    feat_rows = features
    dec_new = empty + jnp.einsum("gnk,ngd->gkd", feat_rows, suffix_piece, precision=HIGHEST)
    gate = jnp.einsum("ngd,gkd->gnk", suffix_piece, dec_weight, precision=HIGHEST) * slopes
    enc_new = empty + jnp.einsum("gnk,nd->gkd", gate, gathered, precision=HIGHEST)
    return (enc_new, dec_new)


def solution(mesh):
    in_specs = (P("feat", None), P("prefix", "feat", None), P("prefix", "feat", None))
    out_specs = (P("prefix", "feat", None), P("prefix", "feat", None))
    return jax.shard_map(
        per_device, mesh=mesh, in_specs=in_specs, out_specs=out_specs, check_vma=False
    )
```

profile of v0, /device:TPU:1, one launch (start us, length us, event | category | flops | bytes accessed | tf_op | source)
XLA Modules:
  0.0 425.4 jit_solution(15453496965193077454)
XLA Ops:
  8.0 58.4 %all-gather.7.cloned.1.call-done = f32[1024,1152]{1,0:T(8,128)} async-done(((f32[32,1152]{1,0:T(8,128)}), f32[1024,1152]{1,0:T(8,128)}) %all-gather.7.cloned.1.call-update) | async-done | bytes 4718608 | tf_op jit(solution)/shard_map/all_gather | solution.py:40
  66.4 12.5 %fusion.2 = f32[2,288,1024]{2,1,0:T(8,128)S(1)} fusion(f32[2,288,1152]{2,1,0:T(8,128)} %param.8, f32[1024,1152]{1,0:T(8,128)} %all-gather.7.cloned.1.call-done), kind=kOutput, calls=%fused_computation.6 | convolution fusion | flops 8153726976 | bytes 9732096 | tf_op jit(solution)/shard_map/nd,gkd->gnk/dot_general | solution.py:42
  78.9 1.4 copy-done.2
  80.3 19.8 %convolution_bitcast_fusion = f32[1024,2,1152]{2,0,1:T(8,128)} fusion(f32[2,288,1152]{2,1,0:T(8,128)S(1)} %copy-done, f32[2,288,1024]{2,1,0:T(8,128)S(1)} %fusion.2), kind=kOutput, calls=%fused_computation.3 | convolution fusion | flops 8158445568 | bytes 14450688 | tf_op jit(solution)/shard_map/gnk,gkd->ngd/dot_general | solution.py:49
  100.1 9.6 %copy.8 = f32[1024,2,1152]{0,2,1:T(8,128)} copy(f32[1024,2,1152]{2,0,1:T(8,128)} %convolution_bitcast_fusion) | data formatting | bytes 18874368 | tf_op jit(solution)/shard_map/gnk,gkd->ngd/transpose | solution.py:49
  109.8 9.6 %copy.13 = f32[1024,2304]{1,0:T(8,128)} copy(f32[1024,2304]{0,1:T(8,128)} %bitcast.55) | data formatting | bytes 18874368
  119.5 100.5 %reduce-scatter.4.cloned.1.call-done = f32[32,2304]{1,0:T(8,128)} async-done(((f32[1024,2304]{1,0:T(8,128)}), f32[32,2304]{1,0:T(8,128)}) %reduce-scatter.4.cloned.1.call-update) | async-done | bytes 294928
  219.9 2.3 copy.14
  222.3 1.4 reduce_sum.18
  224.7 1.6 copy.10
  226.3 33.4 %all-gather.11.cloned.1.call-done = f32[256,1152]{1,0:T(8,128)} async-done(((f32[32,1152]{1,0:T(8,128)}), f32[256,1152]{1,0:T(8,128)}) %all-gather.11.cloned.1.call-update) | async-done | bytes 1179664 | tf_op jit(solution)/shard_map/all_gather | solution.py:11
  259.7 7.8 %while.30 = (s32[]{:T(128)}, f32[32,1152]{1,0:T(8,128)S(1)}, s32[]{:T(128)}, f32[8,32,1152]{2,1,0:T(8,128)}, s32[]{:T(128)}, /*index=5*/s32[]{:T(128)}) while((s32[]{:T(128)}, f32[32,1152]{1,0:T(8,128)S(1)}, s32[]{:T(128)}, f32[8,32,1152]{2,1,0:T(8,128)}, s32[]{:T(128)}, /*index=5*/s32[]{:T(128)}) %tuple.89), condition=%wide.region_3.4_spmd.clone, body=%wide.region_2.3_spmd.clone.sunk | while | flops 110596 | bytes 442461 | solution.py:20
  260.7 1.0 add_select_fusion.4
  261.7 1.0 add_select_fusion.4
  262.6 1.0 add_select_fusion.4
  263.6 1.0 add_select_fusion.4
  264.6 1.0 add_select_fusion.4
  265.6 1.0 add_select_fusion.4
  266.6 1.0 add_select_fusion.4
  268.6 12.6 %fusion.30 = f32[32,2,1152]{2,0,1:T(8,128)S(1)} fusion(f32[32,2,1152]{2,0,1:T(8,128)S(1)} %rev.7), kind=kOutput, calls=%fused_computation.36 | output fusion | flops 73728 | bytes 589824 | tf_op jit(solution)/shard_map/jit(cumsum)/reduce_window_sum | solution.py:35
  281.1 24.7 %all-gather.13.cloned.1.call-done = f32[256,1152]{1,0:T(8,128)} async-done(((f32[32,1152]{1,0:T(8,128)}), f32[256,1152]{1,0:T(8,128)}) %all-gather.13.cloned.1.call-update) | async-done | bytes 1179664 | tf_op jit(solution)/shard_map/all_gather | solution.py:11
  305.9 7.9 %while.31 = (s32[]{:T(128)}, f32[32,1152]{1,0:T(8,128)S(1)}, s32[]{:T(128)}, f32[8,32,1152]{2,1,0:T(8,128)}, s32[]{:T(128)}, /*index=5*/s32[]{:T(128)}, s32[]{:T(128)}, s32[]{:T(128)}) while((s32[]{:T(128)}, f32[32,1152]{1,0:T(8,128)S(1)}, s32[]{:T(128)}, f32[8,32,1152]{2,1,0:T(8,128)}, s32[]{:T(128)}, /*index=5*/s32[]{:T(128)}, ...), condition=%wide.region_7.8_spmd.clone, body=%wide.region_6.7_spmd.clone.sunk | while | flops 110600 | bytes 442523 | solution.py:20
  306.8 1.0 add_select_fusion.5
  307.8 1.0 add_select_fusion.5
  308.8 1.0 add_select_fusion.5
  309.8 1.0 add_select_fusion.5
  310.8 1.0 add_select_fusion.5
  312.8 1.0 add_select_fusion.5
  314.5 64.2 %all-gather.9.cloned.1.call-done = f32[1024,2,1152]{2,0,1:T(8,128)} async-done(((f32[32,2,1152]{2,0,1:T(8,128)}), f32[1024,2,1152]{2,0,1:T(8,128)}) %all-gather.9.cloned.1.call-update) | async-done | bytes 9437200 | tf_op jit(solution)/shard_map/all_gather | solution.py:58
  378.7 13.4 %fusion.31 = f32[2,1024,288]{1,2,0:T(8,128)S(1)} fusion(f32[1024,2,1152]{2,0,1:T(8,128)} %all-gather.9.cloned.1.call-done, f32[2,288,1152]{2,1,0:T(8,128)S(1)} %copy-done), kind=kOutput, calls=%fused_computation.37 | convolution fusion | flops 8153726976 | bytes 14450688 | tf_op jit(solution)/shard_map/ngd,gkd->gnk/dot_general | solution.py:61
  392.1 12.7 %fusion.18 = f32[2,288,1152]{2,1,0:T(8,128)} fusion(f32[1024,2,1152]{2,0,1:T(8,128)S(1)} %copy-done.1, f32[2,288,1024]{2,1,0:T(8,128)S(1)} %copy-done.3), kind=kOutput, calls=%fused_computation.25 | convolution fusion | flops 8158445568 | bytes 14450688 | tf_op jit(solution)/shard_map/gnk,ngd->gkd/dot_general | solution.py:60
  404.8 13.8 %fusion = f32[2,288,1152]{2,1,0:T(8,128)} fusion(f32[1024,1152]{1,0:T(8,128)} %all-gather.7.cloned.1.call-done, f32[2,1024,288]{1,2,0:T(8,128)S(1)} %fusion.31, f32[2,288,1024]{2,1,0:T(8,128)S(1)} %copy-done.3), kind=kOutput, calls=%fused_computation.4 | convolution fusion | flops 8156676096 | bytes 12091392 | tf_op jit(solution)/shard_map/gnk,nd->gkd/dot_general | solution.py:62
  (28 shorter events, 6.4 us)
Async XLA Ops:
  7.2 73.2 %copy-start = (f32[2,288,1152]{2,1,0:T(8,128)S(1)}, f32[2,288,1152]{2,1,0:T(8,128)}, u32[]{:S(2)}) copy-start(f32[2,288,1152]{2,1,0:T(8,128)} %param.9) | copy-start | bytes 7962628
  7.2 59.2 %all-gather.7.cloned.1.call-start = ((), (), s32[]{:S(2)}) async-start(), calls=%async_computation.1 | async-start | bytes 4866048 | tf_op jit(solution)/shard_map/all_gather | solution.py:40
  7.9 212.0 %reduce-scatter.4.cloned.1.call-start = ((), (), s32[]{:S(2)}) async-start(), calls=%async_computation.5 | async-start | bytes 9732096
  78.9 1.4 copy-start.2
  119.4 140.3 %all-gather.11.cloned.1.call-start = ((), (), s32[]{:S(2)}) async-start(), calls=%async_computation.3 | async-start | bytes 1327104 | tf_op jit(solution)/shard_map/all_gather | solution.py:11
  223.7 43.8 %copy-start.4 = (f32[32,1152]{1,0:T(8,128)S(1)}, f32[32,1152]{1,0:T(8,128)}, u32[]{:S(2)}) copy-start(f32[32,1152]{1,0:T(8,128)} %param.7) | copy-start | bytes 442372
  224.6 81.2 %all-gather.13.cloned.1.call-start = ((), (), s32[]{:S(2)}) async-start(), calls=%async_computation.4 | async-start | bytes 1327104 | tf_op jit(solution)/shard_map/all_gather | solution.py:11
  268.5 110.2 %all-gather.9.cloned.1.call-start = ((), (), s32[]{:S(2)}) async-start(), calls=%async_computation.2 | async-start | bytes 9732096 | tf_op jit(solution)/shard_map/all_gather | solution.py:58
  378.7 13.4 %copy-start.1 = (f32[1024,2,1152]{2,0,1:T(8,128)S(1)}, f32[1024,2,1152]{2,0,1:T(8,128)}, u32[]{:S(2)}) copy-start(f32[1024,2,1152]{2,0,1:T(8,128)} %all-gather.9.cloned.1.call-done) | copy-start | bytes 28311556
  378.7 13.4 %copy-start.3 = (f32[2,288,1024]{2,1,0:T(8,128)S(1)}, f32[2,288,1024]{2,1,0:T(8,128)}, u32[]{:S(2)}) copy-start(f32[2,288,1024]{2,1,0:T(8,128)} %copy-done.2) | copy-start | bytes 7077892
Sparse Core Ops, SparseCore 0:
  10.5 55.8 all-gather.6
  119.5 100.3 reduce-scatter.3
  224.7 34.9 all-gather.10
  268.6 37.2 all-gather.12
  314.6 64.0 all-gather.8
where the time goes:
time: 430 us; the launch traced here: 425 us
  waiting for transfers between devices  282 us (66%)
  matrix products  72.2 us (17%)
  other arithmetic  30.9 us (7%)
  local copies, waits for them, and re-layouts  25.5 us (6%)
  between operations  14.1 us (3%)
    unnamed x6, waiting for transfers between devices  101 us
    all_gather x1, waiting for transfers between devices, per_device(): suffix_piece = lax.all_gather(suffix, 'feat', axis=0, tiled=True)  64.2 us
    all_gather x1, waiting for transfers between devices, per_device(): gathered = lax.all_gather(activations, 'feat', axis=0, tiled=True)  58.4 us
    all_gather x2, waiting for transfers between devices, entering(): everything = lax.all_gather(shard, axis)  58.2 us
    dot_general x1, matrix products, per_device(): jnp.einsum('gnk,gkd->ngd', feat_rows, dec_weight, precision=HIGHEST)  19.8 us
    select_n x16, other arithmetic, step(): return jnp.where(reached, new, before)  15.3 us
    unnamed x13, local copies, waits for them, and re-layouts  14.3 us
    dot_general x1, matrix products, per_device(): jnp.einsum('gnk,nd->gkd', gate, gathered, precision=HIGHEST)  13.8 us
  transfers between devices with their start and end apart: 5, of which 5 were waited for; matrix products, arithmetic and copies ran while one was open for 3% of the time, Pallas kernels for 0%

commit v1 on v0

--- a/solution.py
+++ b/solution.py
@@ -55,7 +55,9 @@
     )
     decoded = summed.reshape(summed.shape[0], local_groups, model_width)
     suffix = factor * chain_scan(decoded, activations)
-    suffix_piece = lax.all_gather(suffix, "feat", axis=0, tiled=True)
+    suffix_piece = jnp.concatenate(
+        lax.all_to_all(jnp.stack(lax.axis_size("feat") * [suffix]), "feat", 0, 0), axis=0
+    )
     feat_rows = features
     dec_new = empty + jnp.einsum("gnk,ngd->gkd", feat_rows, suffix_piece, precision=HIGHEST)
     gate = jnp.einsum("ngd,gkd->gnk", suffix_piece, dec_weight, precision=HIGHEST) * slopes

time: 430 us -> 485 us (1.13)
  blocking collectives: 0 us -> 119 us
  waiting for transfers between devices: 282 us -> 230 us
  other arithmetic: 30.9 us -> 18.2 us
  local copies, waits for them, and re-layouts: 25.5 us -> 31 us
  matrix products: 72.2 us -> 66.8 us
    all_to_all x0 -> x1, blocking collectives: none -> 119 us  [per_device(): lax.all_to_all(jnp.stack(lax.axis_size('feat') * [suffix]), 'feat', 0, 0)]
    all_gather x1 -> x0, waiting for transfers between devices: 64.2 us -> none  [per_device(): suffix_piece = lax.all_gather(suffix, 'feat', axis=0, tiled=True)]
    all_gather x2, waiting for transfers between devices: 58.2 us -> 70.2 us  [entering(): everything = lax.all_gather(shard, axis)]
    another operation x1, other arithmetic: 12.6 us -> 0.54 us  [chain_scan(): jnp.cumsum(jnp.flip(errors, 1), axis=1)]
    unnamed x6 -> x5, waiting for transfers between devices: 101 us -> 101 us
    unnamed x13 -> x15, local copies, waits for them, and re-layouts: 14.3 us -> 14.3 us
  transfers between devices with their start and end apart: 5 -> 4, of which waited for: 5 -> 4; matrix products, arithmetic and copies ran while one was open for 3% -> 0% of each run, Pallas kernels for 0% -> 0%
where the time goes in v1:
time: 485 us; the launch traced here: 480 us
  waiting for transfers between devices  230 us (47%)
  blocking collectives  119 us (25%)
  matrix products  66.8 us (14%)
  local copies, waits for them, and re-layouts  31 us (6%)
  other arithmetic  18.2 us (4%)
  between operations  14.1 us (3%)
    all_to_all x1, blocking collectives, per_device(): lax.all_to_all(jnp.stack(lax.axis_size('feat') * [suffix]), 'feat', 0, 0)  119 us
    unnamed x5, waiting for transfers between devices  101 us
    all_gather x2, waiting for transfers between devices, entering(): everything = lax.all_gather(shard, axis)  70.2 us
    all_gather x1, waiting for transfers between devices, per_device(): gathered = lax.all_gather(activations, 'feat', axis=0, tiled=True)  58.4 us
    dot_general x1, matrix products, per_device(): jnp.einsum('gnk,gkd->ngd', feat_rows, dec_weight, precision=HIGHEST)  19.6 us
    select_n x16, other arithmetic, step(): return jnp.where(reached, new, before)  15.3 us
    unnamed x15, local copies, waits for them, and re-layouts  14.3 us
    dot_general x1, matrix products, per_device(): jnp.einsum('gnk,ngd->gkd', feat_rows, suffix_piece, precision=HIGHEST)  13.1 us
  transfers between devices with their start and end apart: 4, of which 4 were waited for; matrix products, arithmetic and copies ran while one was open for 0% of the time, Pallas kernels for 0%

profile of v1, /device:TPU:1, one launch (start us, length us, event | category | flops | bytes accessed | tf_op | source)
XLA Modules:
  0.0 479.8 jit_solution(15696266315157196767)
XLA Ops:
  8.0 58.4 %all-gather.6.cloned.1.call-done = f32[1024,1152]{1,0:T(8,128)} async-done(((f32[32,1152]{1,0:T(8,128)}), f32[1024,1152]{1,0:T(8,128)}) %all-gather.6.cloned.1.call-update) | async-done | bytes 4718608 | tf_op jit(solution)/shard_map/all_gather | solution.py:40
  66.4 12.5 %fusion.2 = f32[2,288,1024]{2,1,0:T(8,128)S(1)} fusion(f32[2,288,1152]{2,1,0:T(8,128)} %param.8, f32[1024,1152]{1,0:T(8,128)} %all-gather.6.cloned.1.call-done), kind=kOutput, calls=%fused_computation.6 | convolution fusion | flops 8153726976 | bytes 9732096 | tf_op jit(solution)/shard_map/nd,gkd->gnk/dot_general | solution.py:42
  78.9 1.4 copy-done.1
  80.3 19.6 %convolution_bitcast_fusion = f32[1024,2,1152]{2,0,1:T(8,128)} fusion(f32[2,288,1152]{2,1,0:T(8,128)S(1)} %copy-done, f32[2,288,1024]{2,1,0:T(8,128)S(1)} %fusion.2), kind=kOutput, calls=%fused_computation.3 | convolution fusion | flops 8158445568 | bytes 14450688 | tf_op jit(solution)/shard_map/gnk,gkd->ngd/dot_general | solution.py:49
  99.9 9.6 %copy.12 = f32[1024,2,1152]{0,2,1:T(8,128)} copy(f32[1024,2,1152]{2,0,1:T(8,128)} %convolution_bitcast_fusion) | data formatting | bytes 18874368 | tf_op jit(solution)/shard_map/gnk,gkd->ngd/transpose | solution.py:49
  109.6 9.6 %copy.18 = f32[1024,2304]{1,0:T(8,128)} copy(f32[1024,2304]{0,1:T(8,128)} %bitcast.58) | data formatting | bytes 18874368
  119.3 100.5 %reduce-scatter.4.cloned.1.call-done = f32[32,2304]{1,0:T(8,128)} async-done(((f32[1024,2304]{1,0:T(8,128)}), f32[32,2304]{1,0:T(8,128)}) %reduce-scatter.4.cloned.1.call-update) | async-done | bytes 294928
  219.7 2.3 copy.19
  222.1 1.4 reduce_sum.18
  224.5 1.6 copy.14
  226.1 33.4 %all-gather.8.cloned.1.call-done = f32[256,1152]{1,0:T(8,128)} async-done(((f32[32,1152]{1,0:T(8,128)}), f32[256,1152]{1,0:T(8,128)}) %all-gather.8.cloned.1.call-update) | async-done | bytes 1179664 | tf_op jit(solution)/shard_map/all_gather | solution.py:11
  259.5 7.8 %while.30 = (s32[]{:T(128)}, f32[32,1152]{1,0:T(8,128)S(1)}, s32[]{:T(128)}, f32[8,32,1152]{2,1,0:T(8,128)}, s32[]{:T(128)}, /*index=5*/s32[]{:T(128)}) while((s32[]{:T(128)}, f32[32,1152]{1,0:T(8,128)S(1)}, s32[]{:T(128)}, f32[8,32,1152]{2,1,0:T(8,128)}, s32[]{:T(128)}, /*index=5*/s32[]{:T(128)}) %tuple.87), condition=%wide.region_3.4_spmd.clone, body=%wide.region_2.3_spmd.clone.sunk | while | flops 110596 | bytes 442461 | solution.py:20
  260.5 1.0 add_select_fusion.4
  261.5 1.0 add_select_fusion.4
  262.4 1.0 add_select_fusion.4
  263.4 1.0 add_select_fusion.4
  264.4 1.0 add_select_fusion.4
  266.4 1.0 add_select_fusion.4
  268.8 36.8 %all-gather.10.cloned.1.call-done = f32[256,1152]{1,0:T(8,128)} async-done(((f32[32,1152]{1,0:T(8,128)}), f32[256,1152]{1,0:T(8,128)}) %all-gather.10.cloned.1.call-update) | async-done | bytes 1179664 | tf_op jit(solution)/shard_map/all_gather | solution.py:11
  305.6 7.9 %while.31 = (s32[]{:T(128)}, f32[32,1152]{1,0:T(8,128)S(1)}, s32[]{:T(128)}, f32[8,32,1152]{2,1,0:T(8,128)}, s32[]{:T(128)}, /*index=5*/s32[]{:T(128)}, s32[]{:T(128)}, s32[]{:T(128)}) while((s32[]{:T(128)}, f32[32,1152]{1,0:T(8,128)S(1)}, s32[]{:T(128)}, f32[8,32,1152]{2,1,0:T(8,128)}, s32[]{:T(128)}, /*index=5*/s32[]{:T(128)}, ...), condition=%wide.region_7.8_spmd.clone, body=%wide.region_6.7_spmd.clone.sunk | while | flops 110600 | bytes 442523 | solution.py:20
  306.6 1.0 add_select_fusion.5
  307.6 1.0 add_select_fusion.5
  308.6 1.0 add_select_fusion.5
  309.6 1.0 add_select_fusion.5
  311.6 1.0 add_select_fusion.5
  312.6 1.0 add_select_fusion.5
  313.6 1.1 stack.2
  314.7 119.4 %all_to_all.5 = f32[32,32,2,1152]{3,1,2,0:T(8,128)} all-to-all(f32[32,32,2,1152]{3,1,2,0:T(8,128)S(1)} %stack.2), channel_id=1, replica_groups=mesh['prefix'=8,'feat'=32] {'feat'}, dimensions={0} | all-to-all | bytes 18874368 | tf_op jit(solution)/shard_map/all_to_all | solution.py:59
  434.1 4.3 copy.15
  438.4 10.1 %fusion.31 = f32[2,1024,288]{1,2,0:T(8,128)S(1)} fusion(f32[1024,2,1152]{2,0,1:T(8,128)S(1)} %bitcast.56, f32[2,288,1152]{2,1,0:T(8,128)S(1)} %copy-done), kind=kOutput, calls=%fused_computation.37 | convolution fusion | flops 8153726976 | bytes 14450688 | tf_op jit(solution)/shard_map/ngd,gkd->gnk/dot_general | solution.py:63
  448.5 13.1 %fusion.18 = f32[2,288,1152]{2,1,0:T(8,128)} fusion(f32[1024,2,1152]{2,0,1:T(8,128)S(1)} %bitcast.57, f32[2,288,1024]{2,1,0:T(8,128)S(1)} %copy-done.2), kind=kOutput, calls=%fused_computation.25 | convolution fusion | flops 8158445568 | bytes 14450688 | tf_op jit(solution)/shard_map/gnk,ngd->gkd/dot_general | solution.py:62
  461.6 11.5 %fusion = f32[2,288,1152]{2,1,0:T(8,128)} fusion(f32[1024,1152]{1,0:T(8,128)S(1)} %bitcast.62, f32[2,1024,288]{1,2,0:T(8,128)S(1)} %fusion.31, f32[2,288,1024]{2,1,0:T(8,128)S(1)} %copy-done.2), kind=kOutput, calls=%fused_computation.4 | convolution fusion | flops 8156676096 | bytes 12091392 | tf_op jit(solution)/shard_map/gnk,nd->gkd/dot_general | solution.py:64
  (31 shorter events, 7.1 us)
Async XLA Ops:
  7.2 73.2 %copy-start = (f32[2,288,1152]{2,1,0:T(8,128)S(1)}, f32[2,288,1152]{2,1,0:T(8,128)}, u32[]{:S(2)}) copy-start(f32[2,288,1152]{2,1,0:T(8,128)} %param.9) | copy-start | bytes 7962628
  7.2 59.2 %all-gather.6.cloned.1.call-start = ((), (), s32[]{:S(2)}) async-start(), calls=%async_computation.2 | async-start | bytes 4866048 | tf_op jit(solution)/shard_map/all_gather | solution.py:40
  7.9 211.8 %reduce-scatter.4.cloned.1.call-start = ((), (), s32[]{:S(2)}) async-start(), calls=%async_computation.5 | async-start | bytes 9732096
  78.9 1.4 copy-start.1
  119.2 140.3 %all-gather.8.cloned.1.call-start = ((), (), s32[]{:S(2)}) async-start(), calls=%async_computation.3 | async-start | bytes 1327104 | tf_op jit(solution)/shard_map/all_gather | solution.py:11
  223.5 43.8 %copy-start.3 = (f32[32,1152]{1,0:T(8,128)S(1)}, f32[32,1152]{1,0:T(8,128)}, u32[]{:S(2)}) copy-start(f32[32,1152]{1,0:T(8,128)} %param.7) | copy-start | bytes 442372
  224.4 81.3 %all-gather.10.cloned.1.call-start = ((), (), s32[]{:S(2)}) async-start(), calls=%async_computation.4 | async-start | bytes 1327104 | tf_op jit(solution)/shard_map/all_gather | solution.py:11
  438.4 10.1 %copy-start.2 = (f32[2,288,1024]{2,1,0:T(8,128)S(1)}, f32[2,288,1024]{2,1,0:T(8,128)}, u32[]{:S(2)}) copy-start(f32[2,288,1024]{2,1,0:T(8,128)} %copy-done.1) | copy-start | bytes 7077892
  438.4 23.2 %slice-start = ((s8[4718592]{0:T(1024)(128)(4,1)}), s8[4194304]{0:T(1024)(128)(4,1)S(1)}, s32[]{:S(2)}) async-start(s8[4718592]{0:T(1024)(128)(4,1)} %bitcast.61), calls=%async_computation.6 | async-start | bytes 8388608
  448.5 13.1 %slice-start.1 = ((s8[4718592]{0:T(1024)(128)(4,1)}), s8[524288]{0:T(1024)(128)(4,1)S(1)}, s32[]{:S(2)}) async-start(s8[4718592]{0:T(1024)(128)(4,1)} %bitcast.61), calls=%async_computation.7 | async-start | bytes 1048576
Sparse Core Ops, SparseCore 0:
  10.5 55.8 all-gather.5
  119.3 100.3 reduce-scatter.3
  224.5 34.9 all-gather.7
  268.4 37.2 all-gather.9
